TPU v7x, 128 devices: a whole 4x4x4 slice. The times are simulated.
128 devices in a mesh: sens: 4 (over y_hi, core), par: 32 (over y_lo, x, z).
Axes of the slice: x: 4, y: 4 (y_hi: 2, y_lo: 2; y = y_hi * 2 + y_lo), z: 4, core: 2. Of those that a mesh axis runs over, the one named last changes fastest.
Arguments:
- data: bfloat16 [32, 600, 420], P(None, 'sens'), may hold values from -6 to 6
- green: bfloat16 [64, 600, 2, 4096], P(None, 'sens', None, 'par'), may hold values from -0.1875 to 0.1875
- freqs: int32 [64], replicated, may hold values from 1 to 209, as said below
- sensor_order: int32 [600], P('sens'), may hold values from 0 to 599, each once
- kappa: float32 [32, 128], P('par'), may hold values from 0.05 to 0.5
- theta: float32 [32, 128], P('par'), may hold values from 0.5 to 2
Outputs:
- prior_field: bfloat16 [32, 420, 32, 128], P('sens', None, 'par')
Inputs may be any that keep to these rules, and one draw needn't show every extreme that they name: `freqs`: distinct; both 1 and 209 appear. `sensor_order`: each sensor fills exactly one slot.
All inputs are finite; a program needn't handle non-finite values.
Results may differ from a plain program's by a relative error of at most 0.015.
Values may be sent and summed in bfloat16 or wider, within the bound.
No kernel may reach another device: no remote copies, remote signals or barrier semaphores. Data moves between devices by JAX's collectives and lax.ppermute only.
A program may use at most 64 MiB of HBM per device.

v0:
```python
import math

import jax
import jax.numpy as jnp
from jax import lax
from jax.experimental import pallas as pl
from jax.experimental.pallas import tpu as pltpu
from jax.sharding import PartitionSpec as P

NT = 420
K = 64
R = 32
ROWS = 32
SWEEPS = 6
SENS = 4
PAR = 32
HERE = 150
PAD = 152
WINDOWS = (0, 128, 344, 472, 256)
BLOCK = 32 * len(WINDOWS)
CHUNK = 80
UNROLL = 16
PIECES = -(-HERE // CHUNK)
AXES = ("sens", "par")
LOWER, UPPER = 0.05, 16.5
f32, bf16, i32 = jnp.float32, jnp.bfloat16, jnp.int32
VMEM = pl.BlockSpec(memory_space=pltpu.VMEM)
SMEM = pl.BlockSpec(memory_space=pltpu.SMEM)
HBM = pl.BlockSpec(memory_space=pltpu.HBM)
NT_DIMS = (((1,), (1,)), ((), ()))
TN_DIMS = (((0,), (0,)), ((), ()))


def iota(shape, dim):
    return lax.broadcasted_iota(i32, shape, dim)


def chebyshev_series():
    d, c = 0.5 * (UPPER + LOWER), 0.5 * (UPPER - LOWER)
    values = []
    for m in range(SWEEPS):
        lam = d - c * math.cos(math.pi * (m + 0.5) / SWEEPS)
        x, res, dirn, alpha = 0.0, 1.0, 0.0, 1.0 / d
        for i in range(SWEEPS):
            beta = 0.0
            if i > 0:
                beta = 0.5 * (c * alpha) ** 2 if i == 1 else (c * alpha / 2.0) ** 2
                alpha = 1.0 / (d - beta / alpha)
            dirn = res + beta * dirn
            x = x + alpha * dirn
            res = res - alpha * lam * dirn
        values.append(x)
    series = [
        2.0 / SWEEPS * sum(v * math.cos(k * math.pi * (m + 0.5) / SWEEPS) for m, v in enumerate(values))
        for k in range(SWEEPS)
    ]
    return [0.5 * series[0]] + series[1:]


def wave(freq, imag, shape, dim):
    t = iota(shape, dim).astype(f32)
    p = t * freq
    m = p - NT * jnp.floor(p * (1.0 / NT))
    m = jnp.where(m < 0, m + NT, m)
    m = jnp.where(m >= NT, m - NT, m)
    m = jnp.where(imag, m + NT // 4, m)
    m = jnp.where(m >= NT, m - NT, m)
    x = (NT // 4 - jnp.minimum(m, NT - m)) * (2.0 * math.pi / NT)
    x2 = x * x
    acc = -1.0 / math.factorial(11) + x2 * (1.0 / math.factorial(13))
    for n, sign in ((9, 1), (7, -1), (5, 1), (3, -1)):
        acc = sign / math.factorial(n) + x2 * acc
    return x + x * x2 * acc


def spectra_kernel(freqs_hbm, data_ref, out_ref, buf, freqs_ref, sems):
    freqs_copy = pltpu.make_async_copy(freqs_hbm, freqs_ref, sems.at[PIECES])
    freqs_copy.start()
    copies = []
    for n in range(PIECES):
        at = pl.ds(n * CHUNK, min(CHUNK, HERE - n * CHUNK))
        copies.append(pltpu.make_async_copy(data_ref.at[at], buf.at[at], sems.at[n]))
        copies[-1].start()
    freqs_copy.wait()
    first = 2 * lax.axis_index("par")
    line = iota((8, NT), 0)
    freq = jnp.where(line < 2, freqs_ref[first], freqs_ref[first + 1]).astype(f32)
    table = wave(freq, (line & 1) == 1, (8, NT), 1) * (1.0 / math.sqrt(NT))
    table = [jnp.broadcast_to(table[j : j + 1], (R, NT)) for j in range(4)]
    table = jnp.concatenate(table, axis=0).astype(bf16)
    own = (iota((R, 128), 1) & 31) == iota((R, 128), 0)
    own = jnp.where(own, 1.0, 0.0).astype(f32).reshape(1, 4, 8, 128)
    fold = (iota((CHUNK, CHUNK * 8), 1) >> 3) == iota((CHUNK, CHUNK * 8), 0)
    fold = jnp.where(fold, 1.0, 0.0).astype(bf16)
    for n, copy in enumerate(copies):
        copy.wait()
        count = min(CHUNK, HERE - n * CHUNK)
        parts = []
        for start in range(0, count, count // 2):
            at = n * CHUNK + start
            x = buf[at : at + count // 2].reshape(count // 2 * R, NT)
            y = lax.dot_general(x, table, NT_DIMS, preferred_element_type=f32)
            y = jnp.sum(y.reshape(count // 2, 4, 8, 128) * own, axis=1)
            parts.append(y.reshape(count // 2 * 8, 128))
        y = jnp.concatenate(parts, axis=0).astype(bf16)
        rows = -(-count // 8) * 8
        y = jnp.dot(fold[:rows, : count * 8], y, preferred_element_type=f32)
        out_ref[n * CHUNK : n * CHUNK + rows, :] = y.astype(bf16)


def split3(x):
    hi = x.astype(bf16).astype(f32)
    mid = (x - hi).astype(bf16).astype(f32)
    return hi, mid, x - hi - mid


def slots_kernel(
    own_ref, core_ref, far_ref, last_ref, order_ref, other_ref, kappa_ref, theta_ref, out_ref
):
    sens = lax.axis_index("sens")
    every = [ref[...] for ref in (own_ref, core_ref, far_ref, last_ref)]
    every = jnp.concatenate(every, axis=0)
    width = 128 * len(WINDOWS)
    at = iota((HERE, width), 1)
    green_row = at
    for n, start in enumerate(WINDOWS):
        green_row = jnp.where((at >> 7) == n, start + (at & 127), green_row)
    slot = jnp.where(green_row >= 2 * HERE, green_row - 2 * HERE, green_row) >> 1
    shared_end = (at >= 4 * 128) & ((at & 127) >= WINDOWS[2] - WINDOWS[4])
    slot = jnp.where(shared_end, -1, slot)
    spread = jnp.where(slot == iota((HERE, width), 0), 1.0, 0.0).astype(bf16)
    lane = iota((R, 128), 1)
    odd = (lane & 1) == 1

    def windows(order):
        block = jnp.where(order >= 150, 1, 0)
        block = jnp.where(order >= 300, 2, block)
        block = jnp.where(order >= 450, 3, block)
        row = (block ^ sens) * PAD + order - HERE * block
        pick = jnp.where(iota((SENS * PAD, HERE), 0) == row, 1.0, 0.0).astype(bf16)
        chosen = lax.dot_general(every, pick, TN_DIMS, preferred_element_type=f32)
        wide = jnp.dot(chosen.astype(bf16), spread, preferred_element_type=f32)
        for n in range(len(WINDOWS)):
            w = wide[:, n * 128 : (n + 1) * 128]
            first = jnp.where(odd, w[32:64], w[0:32])
            second = jnp.where(odd, w[96:128], w[64:96])
            if n < 2:
                v = first
            elif n < 4:
                v = second
            else:
                v = jnp.where(lane < 2 * HERE - WINDOWS[4], first, second)
            zero = (sens & 1) == 0
            yield [jnp.where(zero, v[y : y + 8], v[y + 8 : y + 16]) for y in (0, 16)]

    parts = jnp.zeros((8, 128), f32)
    for n, v in enumerate(split3(kappa_ref[...]) + split3(theta_ref[...])):
        parts = jnp.where(iota((8, 128), 0) == n, v, parts)
    turns = [parts if q == 3 else pltpu.roll(parts, 96 - 32 * q, 1) for q in range(4)]
    rows = []
    for one, two in zip(windows(order_ref[...]), windows(other_ref[...])):
        rows += one + two
    low = iota((8, 128), 1) < 96
    for q in range(4):
        rows[16 + q] = jnp.where(low, rows[16 + q], turns[q])
    block_out = jnp.concatenate(rows, axis=0).astype(bf16)
    for n in range(PAR):
        out_ref[n] = block_out


def prior_kernel(freqs_ref, left_ref, coef_ref, itab_ref, gather_ref):
    flat = left_ref[:, BLOCK - 32 :, :].reshape(PAR * 32, 128)
    lane = iota((32, 128), 1)
    cell = iota((32, 128), 0)
    pick = jnp.where(lane == 96 + cell, 1.0, 0.0).astype(bf16)
    turned = lax.dot_general(pick, flat, NT_DIMS, preferred_element_type=f32).astype(bf16)
    row, to = iota((PAR * 32, 128), 0), iota((PAR * 32, 128), 1)
    here = to == 4 * (row >> 5) + ((row >> 3) & 3)
    part = row & 7
    put = jnp.where(here & (part < 3), 1.0, 0.0).astype(bf16)
    kappa = jnp.dot(turned, put, preferred_element_type=f32)
    put = jnp.where(here & (part >= 3) & (part < 6), 1.0, 0.0).astype(bf16)
    theta = jnp.dot(turned, put, preferred_element_type=f32)
    up, down = lane < 4, lane >= 124
    left = (cell == 0) & ((lane & 3) == 0)
    right = (cell == 31) & ((lane & 3) == 3)
    north = jnp.where(up, theta, pltpu.roll(theta, 4, 1))
    south = jnp.where(down, theta, pltpu.roll(theta, 124, 1))
    back = pltpu.roll(theta, 1, 0)
    west = jnp.where(cell == 0, pltpu.roll(back, 1, 1), back)
    west = jnp.where(left, theta, west)
    ahead = pltpu.roll(theta, 31, 0)
    east = jnp.where(cell == 31, pltpu.roll(ahead, 127, 1), ahead)
    east = jnp.where(right, theta, east)
    north, south, west, east = (0.5 * (theta + v) for v in (north, south, west, east))
    d, c = 0.5 * (UPPER + LOWER), 0.5 * (UPPER - LOWER)
    coefs = [
        (2.0 / c) * (d - (kappa + north + south + west + east)),
        jnp.where(up, 0.0, (2.0 / c) * north),
        jnp.where(down, 0.0, (2.0 / c) * south),
        jnp.where(left, 0.0, (2.0 / c) * west),
        jnp.where(right, 0.0, (2.0 / c) * east),
    ]
    for n, v in enumerate(coefs):
        coef_ref[n] = jnp.broadcast_to(v.reshape(32, 1, 128), (32, 8, 128))
    m, n = iota((256, 1024), 0), iota((256, 1024), 1)
    same = ((m & 7) == (n >> 7)) & ((m >> 3) == ((n & 127) >> 2))
    gather_ref[...] = jnp.where(same, 1.0, 0.0).astype(bf16)
    twice = jnp.where((iota((K, 128), 1) >> 1) == iota((K, 128), 0), 1.0, 0.0).astype(bf16)
    freqs = jnp.broadcast_to(freqs_ref[...].astype(f32), (8, K)).astype(bf16)
    freq = jnp.dot(freqs, twice, preferred_element_type=f32)[0:1]
    imag = (iota((NT, 128), 1) & 1) == 1
    itab_ref[...] = (wave(freq, imag, (NT, 128), 0) * (1.0 / math.sqrt(K))).astype(bf16)


def fetch_kernel(green_hbm, out_ref, sems):
    rows = K * HERE * 2 // 4
    copies = []
    for n in range(4):
        at = pl.ds(n * rows, rows)
        copies.append(pltpu.make_async_copy(green_hbm.at[at], out_ref.at[at], sems.at[n]))
        copies[-1].start()
    for copy in copies:
        copy.wait()


def product_kernel(left_ref, green_ref, swapped_ref, out_hbm, turned_ref, out_ref, sems):
    a, b = iota((128, 128), 0), iota((128, 128), 1)
    turn = jnp.where((a ^ 1) == b, jnp.where((a & 1) == 1, 1.0, -1.0), 0.0).astype(bf16)
    lane = iota((16, 128), 1)
    is_first = lane < 2 * HERE - WINDOWS[4]
    is_second = (lane >= 2 * HERE - WINDOWS[4]) & (lane < WINDOWS[2] - WINDOWS[4])
    zero = jnp.zeros((16, 128), bf16)

    @pl.loop(0, PAR // 8)
    def _(m):
        x = left_ref[pl.ds(8 * m, 8)].reshape(8 * BLOCK, 128)
        x = jnp.dot(x, turn, preferred_element_type=f32).astype(bf16)
        turned_ref[pl.ds(8 * m, 8)] = x.reshape(8, BLOCK, 128)

    def pair(i, base):
        total = []
        for half, green_of in enumerate((green_ref, swapped_ref)):

            def part(n, ref):
                return ref[i, n * 32 + half * 16 : n * 32 + half * 16 + 16, :]

            def both(n, ref):
                return jnp.concatenate([part(n, ref), part(n + 1, ref)], axis=1)

            def green(start, count):
                return green_of[pl.ds(base + start, count), :]

            first = jnp.concatenate([both(0, left_ref), both(0, turned_ref)], axis=0)
            second = jnp.concatenate([both(2, left_ref), both(2, turned_ref)], axis=0)
            s, st = part(4, left_ref), part(4, turned_ref)
            shared = [jnp.where(is_first, v, zero) for v in (s, st)]
            shared += [jnp.where(is_second, v, zero) for v in (s, st)]
            shared = jnp.concatenate(shared, axis=0)
            edge = jnp.dot(shared, green(WINDOWS[4], 128), preferred_element_type=f32)
            one = jnp.dot(first, green(WINDOWS[0], 256), preferred_element_type=f32)
            two = jnp.dot(second, green(WINDOWS[2], 256), preferred_element_type=f32)
            total.append((one + edge[0:32], two + edge[32:64]))
        one, two = (p + q for p, q in zip(*total))
        x = (one[0:16], one[16:32], two[0:16], two[16:32])
        for yh in range(2):
            v = jnp.concatenate([g[8 * yh : 8 * yh + 8] for g in x], axis=0)
            out_ref[yh, i] = v.astype(bf16)

    def piece(m, yh):
        at = pl.ds(16 * m, 16)
        return pltpu.make_async_copy(out_ref.at[yh, at], out_hbm.at[yh, at], sems.at[m, yh])

    @pl.loop(0, PAR // 16)
    def _(m):
        for u in range(16):
            pair(16 * m + u, pl.multiple_of(m * 9600, 16) + 600 * u)
        for yh in range(2):
            piece(m, yh).start()

    for m in range(PAR // 16):
        for yh in range(2):
            piece(m, yh).wait()


def smooth_kernel(moved_ref, coef_ref, gather_ref, out_ref, both, grid, sol):
    series = chebyshev_series()

    def start(b, _):
        v = moved_ref[b].astype(f32) + moved_ref[PAR + b].astype(f32)
        v = v.astype(bf16).astype(f32).reshape(4, 8, 128)
        grid[b] = v
        both[0, b + 1] = series[5] * v
        return 0

    lax.fori_loop(0, PAR, start, 0, unroll=UNROLL)

    def halo(slot):
        both[slot, 0] = pltpu.roll(both[slot, PAR], 1, 2)
        both[slot, PAR + 1] = pltpu.roll(both[slot, 1], 127, 2)

    for k in range(4, -1, -1):
        now, later = k % 2, (k + 1) % 2
        halo(now)

        def step(b, _, k=k, now=now, later=later):
            def coef(n):
                return coef_ref[n, b]

            u = both[now, b + 1]
            v = coef(0) * u
            v = v + coef(1) * pltpu.roll(u, 4, 2)
            v = v + coef(2) * pltpu.roll(u, 124, 2)
            v = v + coef(3) * both[now, b]
            v = v + coef(4) * both[now, b + 2]
            if k == 0:
                v = 0.5 * v
            v = v + series[k] * grid[b]
            if k < 4:
                v = v - both[later, b + 1]
            if k == 0:
                sol[pl.ds(pl.multiple_of(b * 32, 32), 32), :] = v.reshape(32, 128)
            else:
                both[later, b + 1] = v
            return 0

        lax.fori_loop(0, PAR, step, 0, unroll=UNROLL)
    quarter = iota((32, 128), 1) & 3
    for pair in (0, 16):
        turned = []
        for f in range(8):
            column = []
            for g in (pair, pair + 8):
                x = sol[pl.ds(g + f, 32, stride=32), :]
                column += [jnp.where(quarter == q, x, 0.0).astype(bf16) for q in range(4)]
            turned.append(jnp.concatenate(column, axis=0))
        turned = jnp.concatenate(turned, axis=1)
        y = lax.dot_general(gather_ref[...], turned, NT_DIMS, preferred_element_type=f32)
        for n, g in enumerate((pair, pair + 8)):
            v = y[:, n * 128 : (n + 1) * 128].reshape(ROWS, 8, 128)
            out_ref[:, g : g + 8, :] = v.astype(bf16)


def inverse_kernel(back_ref, itab_ref, out_hbm, wide, mixed, ready, sems):
    wide[...] = back_ref[...].reshape(PAR * 32, 128).astype(f32)
    xs = [wide[pl.ds(r, 128, stride=8), :].astype(bf16) for r in range(8)]
    copies = []
    for n, (start, count) in enumerate(((0, 144), (144, 144), (288, 132))):
        at = pl.ds(start, count)
        itab = itab_ref[at, :]
        for r in range(8):
            y = jnp.dot(itab, xs[r], preferred_element_type=f32)
            mixed[pl.ds(8 * start + r, count, stride=8), :] = y
        y = mixed[8 * start : 8 * (start + count), :].astype(bf16)
        ready[at] = y.reshape(count, 8, 128)
        copies.append(pltpu.make_async_copy(ready.at[at], out_hbm.at[at], sems.at[n]))
        copies[-1].start()
    for copy in copies:
        copy.wait()


def call(kernel, out, in_specs, scratch=(), mib=8, to=VMEM):
    many = isinstance(out, (tuple, list))
    return pl.pallas_call(
        kernel,
        out_shape=out,
        in_specs=in_specs,
        out_specs=[to] * len(out) if many else to,
        scratch_shapes=list(scratch),
        compiler_params=pltpu.CompilerParams(vmem_limit_bytes=mib << 20),
    )


def shape(*dims, dtype=bf16):
    return jax.ShapeDtypeStruct(dims, dtype)


def in_hbm(x):
    return pltpu.with_memory_space_constraint(x, pltpu.HBM)


def partner(bit):
    return [(s * PAR + b, (s ^ bit) * PAR + b) for s in range(SENS) for b in range(PAR)]


def local(data, green, freqs, sensor_order, kappa, theta):
    spectra = call(
        spectra_kernel,
        shape(PAD, 128),
        [HBM, HBM],
        [
            pltpu.VMEM((HERE, R, NT), bf16),
            pltpu.SMEM((K,), i32),
            pltpu.SemaphoreType.DMA((PIECES + 1,)),
        ],
        mib=52,
    )(in_hbm(freqs), in_hbm(jnp.transpose(data, (1, 0, 2))))
    table = green.reshape(K * HERE * 2, 128)
    order = sensor_order.reshape(1, HERE)
    far = lax.ppermute(spectra, AXES, partner(2))
    near = lax.ppermute(spectra, AXES, partner(1))
    fetch = [pltpu.SemaphoreType.DMA((4,))]
    here = call(fetch_kernel, shape(K * HERE * 2, 128), [HBM], fetch)(in_hbm(table))
    far, near, here, order = lax.optimization_barrier((far, near, here, order))
    order_two = lax.ppermute(order, AXES, partner(1))
    last = lax.ppermute(far, AXES, partner(1))
    last, order_two, here = lax.optimization_barrier((last, order_two, here))
    swapped = lax.ppermute(here, AXES, partner(1))
    sent = call(slots_kernel, shape(PAR, BLOCK, 128), [VMEM] * 8)(
        spectra, near, far, last, order, order_two, kappa, theta
    )
    left = lax.all_to_all(sent, "par", 0, 0, tiled=True)
    coef, itab, gather = call(
        prior_kernel,
        [shape(5, 32, 8, 128, dtype=f32), shape(NT, 128), shape(256, 1024)],
        [VMEM, VMEM],
    )(freqs.reshape(1, K), left)
    summed = call(
        product_kernel,
        shape(2, PAR, 32, 128),
        [VMEM] * 3,
        [
            pltpu.VMEM((PAR, BLOCK, 128), bf16),
            pltpu.VMEM((2, PAR, 32, 128), bf16),
            pltpu.SemaphoreType.DMA((PAR // 16, 2)),
        ],
        to=HBM,
    )(left, here, swapped).reshape(2 * PAR, 32, 128)
    groups = [[(2 * y + c) * PAR + b for y in range(2) for b in range(PAR)] for c in range(2)]
    moved = lax.all_to_all(summed, AXES, 0, 0, tiled=True, axis_index_groups=groups)
    smooth = call(
        smooth_kernel,
        shape(ROWS, 32, 128),
        [VMEM] * 3,
        [
            pltpu.VMEM((2, PAR + 2, 4, 8, 128), f32),
            pltpu.VMEM((PAR, 4, 8, 128), f32),
            pltpu.VMEM((PAR * 32, 128), f32),
        ],
    )(moved, coef, gather)
    back = lax.all_to_all(smooth, "par", 0, 0, tiled=True)
    out = call(
        inverse_kernel,
        shape(NT, 8, 128),
        [VMEM, VMEM],
        [
            pltpu.VMEM((PAR * 32, 128), f32),
            pltpu.VMEM((NT * 8, 128), f32),
            pltpu.VMEM((NT, 8, 128), bf16),
            pltpu.SemaphoreType.DMA((3,)),
        ],
        to=HBM,
    )(back, itab)
    return jnp.transpose(out, (1, 0, 2)).reshape(8, NT, 1, 128)


def solution(mesh):
    placed = (
        P(None, "sens", None),
        P(None, "sens", None, "par"),
        P(),
        P("sens"),
        P("par", None),
        P("par", None),
    )
    return jax.shard_map(
        local, mesh=mesh, in_specs=placed, out_specs=P("sens", None, "par", None), check_vma=False
    )
```

profile of v0, /device:TPU:0, one launch (start us, length us, event | category | flops | bytes accessed | tf_op | source)
XLA Modules:
  0.0 81.4 jit_solution(201027738184427106)
XLA Ops:
  0.0 3.7 %shard_map.64.own_ref = bf16[152,128]{1,0:T(8,128)(2,1)S(1)} custom-call(s32[64]{0:T(128)} %freqs_hbm.1, bf16[150,32,420]{2,1,0:T(8,128)(2,1)} %bitcast.13), custom_call_target="tpu_custom_call" | custom-call | tf_op jit(solution)/shard_map/pallas_call | solution.py:387
  3.7 3.4 %collective-permute-start = (bf16[152,128]{1,0:T(8,128)(2,1)S(1)}, bf16[152,128]{1,0:T(8,128)(2,1)S(1)}, u32[]{:S(2)}, u32[]{:S(2)}) collective-permute-start(bf16[152,128]{1,0:T(8,128)(2,1)S(1)} %shard_map.64.own_ref), channel_id=1, source_target_pairs={{0,64},{1,65},{2,66},{3,67},{4,68},{5,69},{6,70},{7,71},{8,72},{9,... | collective-permute-start | bytes 116744 | tf_op jit(solution)/shard_map/ppermute | solution.py:400
  7.1 0.0 collective-permute-start.1
  7.1 2.5 %shard_map.65.green_ref = bf16[19200,128]{1,0:T(8,128)(2,1)S(1)} custom-call(bf16[19200,128]{1,0:T(8,128)(2,1)} %bitcast.14), custom_call_target="tpu_custom_call" | custom-call | tf_op jit(solution)/shard_map/pallas_call | solution.py:403
  9.6 0.0 collective-permute-done.far_ref
  9.6 0.0 collective-permute-done.1.core_ref
  9.6 0.6 collective-permute-start.2
  10.2 0.0 copy-done.1
  10.2 0.1 collective-permute-start.3
  10.3 1.1 %collective-permute-done.3.other_ref = s32[1,150]{1,0:T(1,128)S(1)} collective-permute-done((s32[1,150]{1,0:T(1,128)S(1)}, s32[1,150]{1,0:T(1,128)S(1)}, u32[]{:S(2)}, u32[]{:S(2)}) %collective-permute-start.3) | collective-permute-done | bytes 632 | tf_op jit(solution)/shard_map/ppermute | solution.py:405
  11.3 0.0 collective-permute-done.2.last_ref
  11.3 0.2 collective-permute-start.4
  11.5 0.0 copy-done.2
  11.5 0.0 copy-done.3
  11.5 0.8 shard_map.66
  12.3 29.1 %all_to_all.15.left_ref = bf16[32,160,128]{2,1,0:T(8,128)(2,1)S(1)} all-to-all(bf16[32,160,128]{2,1,0:T(8,128)(2,1)S(1)} %shard_map.66), channel_id=1, replica_groups=mesh['sens'=4,'par'=32] {'par'}, dimensions={0} | all-to-all | bytes 2621440 | tf_op jit(solution)/shard_map/all_to_all | solution.py:412
  41.4 0.0 collective-permute-done.4.swapped_ref
  41.4 3.8 %shard_map.67 = bf16[2,32,32,128]{3,2,1,0:T(8,128)(2,1)} custom-call(bf16[32,160,128]{2,1,0:T(8,128)(2,1)S(1)} %all_to_all.15.left_ref, bf16[19200,128]{1,0:T(8,128)(2,1)S(1)} %shard_map.65.green_ref, bf16[19200,128]{1,0:T(8,128)(2,1)S(1)} %collective-permute-done.4.swapped_ref), custom_call_target="tpu_custom_call" | custom-call | tf_op jit(solution)/shard_map/pallas_call | solution.py:418
  45.2 6.9 %all-to-all-start.1 = ((bf16[64,32,128]{2,1,0:T(8,128)(2,1)}), bf16[64,32,128]{2,1,0:T(8,128)(2,1)S(1)}, u32[]{:S(2)}, u32[]{:S(2)}) async-start(bf16[64,32,128]{2,1,0:T(8,128)(2,1)} %bitcast.3), calls=%async_computation.1 | async-start | bytes 1048576 | tf_op jit(solution)/shard_map/all_to_all | solution.py:430
  52.2 1.0 %shard_map.68 = (f32[5,32,8,128]{3,2,1,0:T(8,128)S(1)}, bf16[420,128]{1,0:T(8,128)(2,1)S(1)}, bf16[256,1024]{1,0:T(8,128)(2,1)S(1)}) custom-call(s32[1,64]{1,0:T(1,128)S(1)} %bitcast.10, bf16[32,160,128]{2,1,0:T(8,128)(2,1)S(1)} %all_to_all.15.left_ref), custom_call_target="tpu_custom_call" | custom-call | tf_op jit(solution)/shard_map/pallas_call | solution.py:413
  53.2 11.1 %all-to-all-done.1.moved_ref = bf16[64,32,128]{2,1,0:T(8,128)(2,1)S(1)} async-done(((bf16[64,32,128]{2,1,0:T(8,128)(2,1)}), bf16[64,32,128]{2,1,0:T(8,128)(2,1)S(1)}, u32[]{:S(2)}, u32[]{:S(2)}) %all-to-all-start.1) | async-done | bytes 524320 | tf_op jit(solution)/shard_map/all_to_all | solution.py:430
  64.3 3.1 %shard_map.69 = bf16[32,32,128]{2,1,0:T(8,128)(2,1)S(1)} custom-call(bf16[64,32,128]{2,1,0:T(8,128)(2,1)S(1)} %all-to-all-done.1.moved_ref, f32[5,32,8,128]{3,2,1,0:T(8,128)S(1)} %get-tuple-element.22.coef_ref, bf16[256,1024]{1,0:T(8,128)(2,1)S(1)} %get-tuple-element.23.gather_ref), custom_call_target="tpu_custom_call" | custom-call | tf_op jit(solution)/shard_map/pallas_call | solution.py:431
  67.5 12.4 %all_to_all.16.back_ref = bf16[32,32,128]{2,1,0:T(8,128)(2,1)S(1)} all-to-all(bf16[32,32,128]{2,1,0:T(8,128)(2,1)S(1)} %shard_map.69), channel_id=1, replica_groups=mesh['sens'=4,'par'=32] {'par'}, dimensions={0} | all-to-all | bytes 524288 | tf_op jit(solution)/shard_map/all_to_all | solution.py:441
  79.9 1.5 %shard_map.70 = bf16[420,8,128]{2,1,0:T(8,128)(2,1)} custom-call(bf16[32,32,128]{2,1,0:T(8,128)(2,1)S(1)} %all_to_all.16.back_ref, bf16[420,128]{1,0:T(8,128)(2,1)S(1)} %get-tuple-element.24.itab_ref), custom_call_target="tpu_custom_call" | custom-call | tf_op jit(solution)/shard_map/pallas_call | solution.py:442
  (5 shorter events, 0.0 us)
Async XLA Ops:
  3.7 5.9 %collective-permute-start = (bf16[152,128]{1,0:T(8,128)(2,1)S(1)}, bf16[152,128]{1,0:T(8,128)(2,1)S(1)}, u32[]{:S(2)}, u32[]{:S(2)}) collective-permute-start(bf16[152,128]{1,0:T(8,128)(2,1)S(1)} %shard_map.64.own_ref), channel_id=1, source_target_pairs={{0,64},{1,65},{2,66},{3,67},{4,68},{5,69},{6,70},{7,71},{8,72},{9,... | collective-permute-start | bytes 116744 | tf_op jit(solution)/shard_map/ppermute | solution.py:400
  7.1 2.5 %collective-permute-start.1 = (bf16[152,128]{1,0:T(8,128)(2,1)S(1)}, bf16[152,128]{1,0:T(8,128)(2,1)S(1)}, u32[]{:S(2)}, u32[]{:S(2)}) collective-permute-start(bf16[152,128]{1,0:T(8,128)(2,1)S(1)} %shard_map.64.own_ref), channel_id=1, source_target_pairs={{0,32},{1,33},{2,34},{3,35},{4,36},{5,37},{6,38},{7,39},{8,40},{9,... | collective-permute-start | bytes 116744 | tf_op jit(solution)/shard_map/ppermute | solution.py:401
  7.1 3.1 %copy-start.1 = (s32[150]{0:T(256)S(1)}, s32[150]{0:T(256)}, u32[]{:S(2)}) copy-start(s32[150]{0:T(256)} %param.9) | copy-start | bytes 1804
  7.1 4.4 %copy-start.2 = (f32[1,128]{1,0:T(1,128)S(1)}, f32[1,128]{1,0:T(1,128)}, u32[]{:S(2)}) copy-start(f32[1,128]{1,0:T(1,128)} %kappa_ref.1) | copy-start | bytes 1540
  7.1 4.4 %copy-start.3 = (f32[1,128]{1,0:T(1,128)S(1)}, f32[1,128]{1,0:T(1,128)}, u32[]{:S(2)}) copy-start(f32[1,128]{1,0:T(1,128)} %theta_ref.1) | copy-start | bytes 1540
  9.6 1.8 %collective-permute-start.2 = (bf16[152,128]{1,0:T(8,128)(2,1)S(1)}, bf16[152,128]{1,0:T(8,128)(2,1)S(1)}, u32[]{:S(2)}, u32[]{:S(2)}) collective-permute-start(bf16[152,128]{1,0:T(8,128)(2,1)S(1)} %collective-permute-done.far_ref), channel_id=1, source_target_pairs={{0,32},{1,33},{2,34},{3,35},{4,36},{5,37},{6,38},{7,39},{8,40},{9,... | collective-permute-start | bytes 116744 | tf_op jit(solution)/shard_map/ppermute | solution.py:406
  10.2 1.2 %collective-permute-start.3 = (s32[1,150]{1,0:T(1,128)S(1)}, s32[1,150]{1,0:T(1,128)S(1)}, u32[]{:S(2)}, u32[]{:S(2)}) collective-permute-start(s32[1,150]{1,0:T(1,128)S(1)} %bitcast.11), channel_id=1, source_target_pairs={{0,32},{1,33},{2,34},{3,35},{4,36},{5,37},{6,38},{7,39},{8,40},{9,... | collective-permute-start | bytes 1808 | tf_op jit(solution)/shard_map/ppermute | solution.py:405
  11.3 30.1 %collective-permute-start.4 = (bf16[19200,128]{1,0:T(8,128)(2,1)S(1)}, bf16[19200,128]{1,0:T(8,128)(2,1)S(1)}, u32[]{:S(2)}, u32[]{:S(2)}) collective-permute-start(bf16[19200,128]{1,0:T(8,128)(2,1)S(1)} %shard_map.65.green_ref), channel_id=1, source_target_pairs={{0,32},{1,33},{2,34},{3,35},{4,36},{5,37},{6,38},{7,39},{8,40},{9,... | collective-permute-start | bytes 14745608 | tf_op jit(solution)/shard_map/ppermute | solution.py:408
  41.4 10.7 %copy-start = (s32[64]{0:T(128)S(1)}, s32[64]{0:T(128)}, u32[]{:S(2)}) copy-start(s32[64]{0:T(128)} %freqs_hbm.1) | copy-start | bytes 772
  45.2 19.1 %all-to-all-start.1 = ((bf16[64,32,128]{2,1,0:T(8,128)(2,1)}), bf16[64,32,128]{2,1,0:T(8,128)(2,1)S(1)}, u32[]{:S(2)}, u32[]{:S(2)}) async-start(bf16[64,32,128]{2,1,0:T(8,128)(2,1)} %bitcast.3), calls=%async_computation.1 | async-start | bytes 1048576 | tf_op jit(solution)/shard_map/all_to_all | solution.py:430
where the time goes:
time: 81.6 us; the launch traced here: 81.4 us
  blocking collectives  41.6 us (51%)
  Pallas kernels  16.3 us (20%)
  waiting for transfers between devices  12.2 us (15%)
  starting transfers between devices  11.2 us (14%)
    all_to_all x1, blocking collectives, local(): left = lax.all_to_all(sent, 'par', 0, 0, tiled=True)  29.1 us
    all_to_all x1, blocking collectives, local(): back = lax.all_to_all(smooth, 'par', 0, 0, tiled=True)  12.4 us
    all_to_all x1, waiting for transfers between devices, local(): lax.all_to_all(summed, AXES, 0, 0, tiled=True, axis_index_groups=groups)  11.1 us
    all_to_all x1, starting transfers between devices, local(): lax.all_to_all(summed, AXES, 0, 0, tiled=True, axis_index_groups=groups)  6.93 us
    pallas_call x1, Pallas kernels, local(): call(product_kernel, shape(2, PAR, 32, 128), [VMEM] * 3, [pltpu.VMEM((PAR...  3.79 us
    pallas_call x1, Pallas kernels, local(): call(spectra_kernel, shape(PAD, 128), [HBM, HBM], [pltpu.VMEM((HERE, R, N...  3.68 us
    ppermute x1, starting transfers between devices, local(): far = lax.ppermute(spectra, AXES, partner(2))  3.39 us
    pallas_call x1, Pallas kernels, local(): call(smooth_kernel, shape(ROWS, 32, 128), [VMEM] * 3, [pltpu.VMEM((2, PAR...  3.13 us
  transfers between devices with their start and end apart: 6, of which 2 were waited for; matrix products, arithmetic and copies ran while one was open for 0% of the time, Pallas kernels for 5%

commit v1 on v0

--- a/solution.py
+++ b/solution.py
@@ -168,7 +168,7 @@
         out_ref[n] = block_out
 
 
-def prior_kernel(freqs_ref, left_ref, coef_ref, itab_ref, gather_ref):
+def coefficients(left_ref, coef_ref):
     flat = left_ref[:, BLOCK - 32 :, :].reshape(PAR * 32, 128)
     lane = iota((32, 128), 1)
     cell = iota((32, 128), 0)
@@ -203,6 +203,9 @@
     ]
     for n, v in enumerate(coefs):
         coef_ref[n] = jnp.broadcast_to(v.reshape(32, 1, 128), (32, 8, 128))
+
+
+def tables(freqs_ref, itab_ref, gather_ref):
     m, n = iota((256, 1024), 0), iota((256, 1024), 1)
     same = ((m & 7) == (n >> 7)) & ((m >> 3) == ((n & 127) >> 2))
     gather_ref[...] = jnp.where(same, 1.0, 0.0).astype(bf16)
@@ -213,18 +216,19 @@
     itab_ref[...] = (wave(freq, imag, (NT, 128), 0) * (1.0 / math.sqrt(K))).astype(bf16)
 
 
-def fetch_kernel(green_hbm, out_ref, sems):
+def fetch_kernel(green_hbm, freqs_ref, out_ref, itab_ref, gather_ref, sems):
     rows = K * HERE * 2 // 4
     copies = []
     for n in range(4):
         at = pl.ds(n * rows, rows)
         copies.append(pltpu.make_async_copy(green_hbm.at[at], out_ref.at[at], sems.at[n]))
         copies[-1].start()
+    tables(freqs_ref, itab_ref, gather_ref)
     for copy in copies:
         copy.wait()
 
 
-def product_kernel(left_ref, green_ref, swapped_ref, out_hbm, turned_ref, out_ref, sems):
+def product_kernel(left_ref, green_ref, swapped_ref, out_ref, turned_ref):
     a, b = iota((128, 128), 0), iota((128, 128), 1)
     turn = jnp.where((a ^ 1) == b, jnp.where((a & 1) == 1, 1.0, -1.0), 0.0).astype(bf16)
     lane = iota((16, 128), 1)
@@ -267,23 +271,14 @@
             v = jnp.concatenate([g[8 * yh : 8 * yh + 8] for g in x], axis=0)
             out_ref[yh, i] = v.astype(bf16)
 
-    def piece(m, yh):
-        at = pl.ds(16 * m, 16)
-        return pltpu.make_async_copy(out_ref.at[yh, at], out_hbm.at[yh, at], sems.at[m, yh])
-
     @pl.loop(0, PAR // 16)
     def _(m):
         for u in range(16):
             pair(16 * m + u, pl.multiple_of(m * 9600, 16) + 600 * u)
-        for yh in range(2):
-            piece(m, yh).start()
-
-    for m in range(PAR // 16):
-        for yh in range(2):
-            piece(m, yh).wait()
-
-
-def smooth_kernel(moved_ref, coef_ref, gather_ref, out_ref, both, grid, sol):
+
+
+def smooth_kernel(moved_ref, left_ref, gather_ref, out_ref, both, grid, sol, coef_ref):
+    coefficients(left_ref, coef_ref)
     series = chebyshev_series()
 
     def start(b, _):
@@ -399,8 +394,12 @@
     order = sensor_order.reshape(1, HERE)
     far = lax.ppermute(spectra, AXES, partner(2))
     near = lax.ppermute(spectra, AXES, partner(1))
-    fetch = [pltpu.SemaphoreType.DMA((4,))]
-    here = call(fetch_kernel, shape(K * HERE * 2, 128), [HBM], fetch)(in_hbm(table))
+    here, itab, gather = call(
+        fetch_kernel,
+        [shape(K * HERE * 2, 128), shape(NT, 128), shape(256, 1024)],
+        [HBM, VMEM],
+        [pltpu.SemaphoreType.DMA((4,))],
+    )(in_hbm(table), freqs.reshape(1, K))
     far, near, here, order = lax.optimization_barrier((far, near, here, order))
     order_two = lax.ppermute(order, AXES, partner(1))
     last = lax.ppermute(far, AXES, partner(1))
@@ -410,21 +409,13 @@
         spectra, near, far, last, order, order_two, kappa, theta
     )
     left = lax.all_to_all(sent, "par", 0, 0, tiled=True)
-    coef, itab, gather = call(
-        prior_kernel,
-        [shape(5, 32, 8, 128, dtype=f32), shape(NT, 128), shape(256, 1024)],
-        [VMEM, VMEM],
-    )(freqs.reshape(1, K), left)
     summed = call(
         product_kernel,
         shape(2, PAR, 32, 128),
         [VMEM] * 3,
         [
             pltpu.VMEM((PAR, BLOCK, 128), bf16),
-            pltpu.VMEM((2, PAR, 32, 128), bf16),
-            pltpu.SemaphoreType.DMA((PAR // 16, 2)),
         ],
-        to=HBM,
     )(left, here, swapped).reshape(2 * PAR, 32, 128)
     groups = [[(2 * y + c) * PAR + b for y in range(2) for b in range(PAR)] for c in range(2)]
     moved = lax.all_to_all(summed, AXES, 0, 0, tiled=True, axis_index_groups=groups)
@@ -436,8 +427,9 @@
             pltpu.VMEM((2, PAR + 2, 4, 8, 128), f32),
             pltpu.VMEM((PAR, 4, 8, 128), f32),
             pltpu.VMEM((PAR * 32, 128), f32),
+            pltpu.VMEM((5, 32, 8, 128), f32),
         ],
-    )(moved, coef, gather)
+    )(moved, left, gather)
     back = lax.all_to_all(smooth, "par", 0, 0, tiled=True)
     out = call(
         inverse_kernel,

time: 81.6 us -> 81.3 us (level)
  blocking collectives: 41.6 us -> 60.6 us
  waiting for transfers between devices: 12.2 us -> 0.83 us
  starting transfers between devices: 11.2 us -> 4.4 us
  Pallas kernels: 16.3 us -> 15.1 us
    all_to_all x0 -> x1, blocking collectives: none -> 18.9 us  [local(): lax.all_to_all(summed, AXES, 0, 0, tiled=True, axis_index_groups=groups)]
    all_to_all x1 -> x0, waiting for transfers between devices: 11.1 us -> none  [local(): lax.all_to_all(summed, AXES, 0, 0, tiled=True, axis_index_groups=groups)]
    all_to_all x1 -> x0, starting transfers between devices: 6.93 us -> none  [local(): lax.all_to_all(summed, AXES, 0, 0, tiled=True, axis_index_groups=groups)]
    pallas_call x2 -> x1, Pallas kernels: 3.48 us -> 2.46 us  [local(): call(fetch_kernel, [shape(K * HERE * 2, 128), shape(NT, 128), shape(256,...]
  transfers between devices with their start and end apart: 6 -> 5, of which waited for: 2 -> 1; matrix products, arithmetic and copies ran while one was open for 0% -> 0% of each run, Pallas kernels for 5% -> 4%
where the time goes in v1:
time: 81.3 us; the launch traced here: 81.1 us
  blocking collectives  60.6 us (75%)
  Pallas kernels  15.1 us (19%)
  starting transfers between devices  4.4 us (5%)
  waiting for transfers between devices  0.83 us (1%)
    all_to_all x1, blocking collectives, local(): left = lax.all_to_all(sent, 'par', 0, 0, tiled=True)  29.3 us
    all_to_all x1, blocking collectives, local(): lax.all_to_all(summed, AXES, 0, 0, tiled=True, axis_index_groups=groups)  18.9 us
    all_to_all x1, blocking collectives, local(): back = lax.all_to_all(smooth, 'par', 0, 0, tiled=True)  12.4 us
    pallas_call x1, Pallas kernels, local(): call(spectra_kernel, shape(PAD, 128), [HBM, HBM], [pltpu.VMEM((HERE, R, N...  3.73 us
    pallas_call x1, Pallas kernels, local(): call(smooth_kernel, shape(ROWS, 32, 128), [VMEM] * 3, [pltpu.VMEM((2, PAR...  3.65 us
    ppermute x1, starting transfers between devices, local(): far = lax.ppermute(spectra, AXES, partner(2))  3.39 us
    pallas_call x1, Pallas kernels, local(): call(product_kernel, shape(2, PAR, 32, 128), [VMEM] * 3, [pltpu.VMEM((PAR...  3.05 us
    pallas_call x1, Pallas kernels, local(): call(fetch_kernel, [shape(K * HERE * 2, 128), shape(NT, 128), shape(256,...  2.46 us
  transfers between devices with their start and end apart: 5, of which 1 were waited for; matrix products, arithmetic and copies ran while one was open for 0% of the time, Pallas kernels for 4%

profile of v1, /device:TPU:0, one launch (start us, length us, event | category | flops | bytes accessed | tf_op | source)
XLA Modules:
  0.0 81.1 jit_solution(8113078354376414494)
XLA Ops:
  0.0 0.0 copy-start
  0.0 3.7 %shard_map.64.own_ref = bf16[152,128]{1,0:T(8,128)(2,1)S(1)} custom-call(s32[64]{0:T(128)} %freqs_hbm.1, bf16[150,32,420]{2,1,0:T(8,128)(2,1)} %bitcast.15), custom_call_target="tpu_custom_call" | custom-call | tf_op jit(solution)/shard_map/pallas_call | solution.py:382
  3.7 0.1 collective-permute-start.1
  3.8 3.4 %collective-permute-start = (bf16[152,128]{1,0:T(8,128)(2,1)S(1)}, bf16[152,128]{1,0:T(8,128)(2,1)S(1)}, u32[]{:S(2)}, u32[]{:S(2)}) collective-permute-start(bf16[152,128]{1,0:T(8,128)(2,1)S(1)} %shard_map.64.own_ref), channel_id=1, source_target_pairs={{0,64},{1,65},{2,66},{3,67},{4,68},{5,69},{6,70},{7,71},{8,72},{9,... | collective-permute-start | bytes 116744 | tf_op jit(solution)/shard_map/ppermute | solution.py:395
  7.2 0.0 copy-done
  7.2 2.5 %shard_map.65 = (bf16[19200,128]{1,0:T(8,128)(2,1)S(1)}, bf16[420,128]{1,0:T(8,128)(2,1)S(1)}, bf16[256,1024]{1,0:T(8,128)(2,1)S(1)}) custom-call(bf16[19200,128]{1,0:T(8,128)(2,1)} %bitcast.14, s32[1,64]{1,0:T(1,128)S(1)} %bitcast.11), custom_call_target="tpu_custom_call" | custom-call | tf_op jit(solution)/shard_map/pallas_call | solution.py:397
  9.7 0.0 collective-permute-done.1.core_ref
  9.7 0.0 collective-permute-done.far_ref
  9.7 0.2 collective-permute-start.2
  9.9 0.0 copy-done.1
  9.9 0.4 collective-permute-start.3
  10.3 0.8 %collective-permute-done.3.other_ref = s32[1,150]{1,0:T(1,128)S(1)} collective-permute-done((s32[1,150]{1,0:T(1,128)S(1)}, s32[1,150]{1,0:T(1,128)S(1)}, u32[]{:S(2)}, u32[]{:S(2)}) %collective-permute-start.3) | collective-permute-done | bytes 632 | tf_op jit(solution)/shard_map/ppermute | solution.py:404
  11.1 0.0 collective-permute-done.2.last_ref
  11.1 0.3 collective-permute-start.4
  11.5 0.0 copy-done.2
  11.5 0.0 copy-done.3
  11.5 0.8 shard_map.66
  12.3 29.3 %all_to_all.15.left_ref = bf16[32,160,128]{2,1,0:T(8,128)(2,1)S(1)} all-to-all(bf16[32,160,128]{2,1,0:T(8,128)(2,1)S(1)} %shard_map.66), channel_id=1, replica_groups=mesh['sens'=4,'par'=32] {'par'}, dimensions={0} | all-to-all | bytes 2621440 | tf_op jit(solution)/shard_map/all_to_all | solution.py:411
  41.6 0.0 collective-permute-done.4.swapped_ref
  41.6 3.1 %shard_map.67 = bf16[2,32,32,128]{3,2,1,0:T(8,128)(2,1)S(1)} custom-call(bf16[32,160,128]{2,1,0:T(8,128)(2,1)S(1)} %all_to_all.15.left_ref, bf16[19200,128]{1,0:T(8,128)(2,1)S(1)} %get-tuple-element.22.green_ref, bf16[19200,128]{1,0:T(8,128)(2,1)S(1)} %collective-permute-done.4.swapped_ref), custom_call_target="tpu_custom_call" | custom-call | tf_op jit(solution)/shard_map/pallas_call | solution.py:412
  44.6 18.9 %all_to_all.16.moved_ref = bf16[64,32,128]{2,1,0:T(8,128)(2,1)S(1)} all-to-all(bf16[64,32,128]{2,1,0:T(8,128)(2,1)S(1)} %bitcast.10), channel_id=1, replica_groups={{0,1,2,3,4,5,6,7,8,9,10,11,12,13,14,15,16,17,18,19,20,21,22,23,24,25,26..., dimensions={0} | all-to-all | bytes 1048576 | tf_op jit(solution)/shard_map/all_to_all | solution.py:421
  63.5 3.6 %shard_map.68 = bf16[32,32,128]{2,1,0:T(8,128)(2,1)S(1)} custom-call(bf16[64,32,128]{2,1,0:T(8,128)(2,1)S(1)} %all_to_all.16.moved_ref, bf16[32,160,128]{2,1,0:T(8,128)(2,1)S(1)} %all_to_all.15.left_ref, bf16[256,1024]{1,0:T(8,128)(2,1)S(1)} %get-tuple-element.23.gather_ref), custom_call_target="tpu_custom_call" | custom-call | tf_op jit(solution)/shard_map/pallas_call | solution.py:422
  67.2 12.4 %all_to_all.17.back_ref = bf16[32,32,128]{2,1,0:T(8,128)(2,1)S(1)} all-to-all(bf16[32,32,128]{2,1,0:T(8,128)(2,1)S(1)} %shard_map.68), channel_id=1, replica_groups=mesh['sens'=4,'par'=32] {'par'}, dimensions={0} | all-to-all | bytes 524288 | tf_op jit(solution)/shard_map/all_to_all | solution.py:433
  79.6 1.5 %shard_map.69 = bf16[420,8,128]{2,1,0:T(8,128)(2,1)} custom-call(bf16[32,32,128]{2,1,0:T(8,128)(2,1)S(1)} %all_to_all.17.back_ref, bf16[420,128]{1,0:T(8,128)(2,1)S(1)} %get-tuple-element.24.itab_ref), custom_call_target="tpu_custom_call" | custom-call | tf_op jit(solution)/shard_map/pallas_call | solution.py:434
  (3 shorter events, 0.0 us)
Async XLA Ops:
  0.0 7.2 %copy-start = (s32[64]{0:T(128)S(1)}, s32[64]{0:T(128)}, u32[]{:S(2)}) copy-start(s32[64]{0:T(128)} %freqs_hbm.1) | copy-start | bytes 772
  0.0 9.9 %copy-start.1 = (s32[150]{0:T(256)S(1)}, s32[150]{0:T(256)}, u32[]{:S(2)}) copy-start(s32[150]{0:T(256)} %param.9) | copy-start | bytes 1804
  0.0 11.5 %copy-start.2 = (f32[1,128]{1,0:T(1,128)S(1)}, f32[1,128]{1,0:T(1,128)}, u32[]{:S(2)}) copy-start(f32[1,128]{1,0:T(1,128)} %kappa_ref.1) | copy-start | bytes 1540
  0.0 11.5 %copy-start.3 = (f32[1,128]{1,0:T(1,128)S(1)}, f32[1,128]{1,0:T(1,128)}, u32[]{:S(2)}) copy-start(f32[1,128]{1,0:T(1,128)} %theta_ref.1) | copy-start | bytes 1540
  3.7 5.9 %collective-permute-start.1 = (bf16[152,128]{1,0:T(8,128)(2,1)S(1)}, bf16[152,128]{1,0:T(8,128)(2,1)S(1)}, u32[]{:S(2)}, u32[]{:S(2)}) collective-permute-start(bf16[152,128]{1,0:T(8,128)(2,1)S(1)} %shard_map.64.own_ref), channel_id=1, source_target_pairs={{0,32},{1,33},{2,34},{3,35},{4,36},{5,37},{6,38},{7,39},{8,40},{9,... | collective-permute-start | bytes 116744 | tf_op jit(solution)/shard_map/ppermute | solution.py:396
  3.8 5.9 %collective-permute-start = (bf16[152,128]{1,0:T(8,128)(2,1)S(1)}, bf16[152,128]{1,0:T(8,128)(2,1)S(1)}, u32[]{:S(2)}, u32[]{:S(2)}) collective-permute-start(bf16[152,128]{1,0:T(8,128)(2,1)S(1)} %shard_map.64.own_ref), channel_id=1, source_target_pairs={{0,64},{1,65},{2,66},{3,67},{4,68},{5,69},{6,70},{7,71},{8,72},{9,... | collective-permute-start | bytes 116744 | tf_op jit(solution)/shard_map/ppermute | solution.py:395
  9.7 1.4 %collective-permute-start.2 = (bf16[152,128]{1,0:T(8,128)(2,1)S(1)}, bf16[152,128]{1,0:T(8,128)(2,1)S(1)}, u32[]{:S(2)}, u32[]{:S(2)}) collective-permute-start(bf16[152,128]{1,0:T(8,128)(2,1)S(1)} %collective-permute-done.far_ref), channel_id=1, source_target_pairs={{0,32},{1,33},{2,34},{3,35},{4,36},{5,37},{6,38},{7,39},{8,40},{9,... | collective-permute-start | bytes 116744 | tf_op jit(solution)/shard_map/ppermute | solution.py:405
  9.9 1.2 %collective-permute-start.3 = (s32[1,150]{1,0:T(1,128)S(1)}, s32[1,150]{1,0:T(1,128)S(1)}, u32[]{:S(2)}, u32[]{:S(2)}) collective-permute-start(s32[1,150]{1,0:T(1,128)S(1)} %bitcast.12), channel_id=1, source_target_pairs={{0,32},{1,33},{2,34},{3,35},{4,36},{5,37},{6,38},{7,39},{8,40},{9,... | collective-permute-start | bytes 1808 | tf_op jit(solution)/shard_map/ppermute | solution.py:404
  11.1 30.4 %collective-permute-start.4 = (bf16[19200,128]{1,0:T(8,128)(2,1)S(1)}, bf16[19200,128]{1,0:T(8,128)(2,1)S(1)}, u32[]{:S(2)}, u32[]{:S(2)}) collective-permute-start(bf16[19200,128]{1,0:T(8,128)(2,1)S(1)} %get-tuple-element.22.green_ref), channel_id=1, source_target_pairs={{0,32},{1,33},{2,34},{3,35},{4,36},{5,37},{6,38},{7,39},{8,40},{9,... | collective-permute-start | bytes 14745608 | tf_op jit(solution)/shard_map/ppermute | solution.py:407

commit v2 on v1

--- a/solution.py
+++ b/solution.py
@@ -168,19 +168,14 @@
         out_ref[n] = block_out
 
 
-def coefficients(left_ref, coef_ref):
+def coefficients(left_ref, put_ref, coef_ref):
     flat = left_ref[:, BLOCK - 32 :, :].reshape(PAR * 32, 128)
     lane = iota((32, 128), 1)
     cell = iota((32, 128), 0)
     pick = jnp.where(lane == 96 + cell, 1.0, 0.0).astype(bf16)
     turned = lax.dot_general(pick, flat, NT_DIMS, preferred_element_type=f32).astype(bf16)
-    row, to = iota((PAR * 32, 128), 0), iota((PAR * 32, 128), 1)
-    here = to == 4 * (row >> 5) + ((row >> 3) & 3)
-    part = row & 7
-    put = jnp.where(here & (part < 3), 1.0, 0.0).astype(bf16)
-    kappa = jnp.dot(turned, put, preferred_element_type=f32)
-    put = jnp.where(here & (part >= 3) & (part < 6), 1.0, 0.0).astype(bf16)
-    theta = jnp.dot(turned, put, preferred_element_type=f32)
+    kappa = jnp.dot(turned, put_ref[0], preferred_element_type=f32)
+    theta = jnp.dot(turned, put_ref[1], preferred_element_type=f32)
     up, down = lane < 4, lane >= 124
     left = (cell == 0) & ((lane & 3) == 0)
     right = (cell == 31) & ((lane & 3) == 3)
@@ -205,7 +200,12 @@
         coef_ref[n] = jnp.broadcast_to(v.reshape(32, 1, 128), (32, 8, 128))
 
 
-def tables(freqs_ref, itab_ref, gather_ref):
+def tables(freqs_ref, itab_ref, gather_ref, put_ref):
+    row, to = iota((PAR * 32, 128), 0), iota((PAR * 32, 128), 1)
+    here = to == 4 * (row >> 5) + ((row >> 3) & 3)
+    part = row & 7
+    put_ref[0] = jnp.where(here & (part < 3), 1.0, 0.0).astype(bf16)
+    put_ref[1] = jnp.where(here & (part >= 3) & (part < 6), 1.0, 0.0).astype(bf16)
     m, n = iota((256, 1024), 0), iota((256, 1024), 1)
     same = ((m & 7) == (n >> 7)) & ((m >> 3) == ((n & 127) >> 2))
     gather_ref[...] = jnp.where(same, 1.0, 0.0).astype(bf16)
@@ -216,14 +216,14 @@
     itab_ref[...] = (wave(freq, imag, (NT, 128), 0) * (1.0 / math.sqrt(K))).astype(bf16)
 
 
-def fetch_kernel(green_hbm, freqs_ref, out_ref, itab_ref, gather_ref, sems):
+def fetch_kernel(green_hbm, freqs_ref, out_ref, itab_ref, gather_ref, put_ref, sems):
     rows = K * HERE * 2 // 4
     copies = []
     for n in range(4):
         at = pl.ds(n * rows, rows)
         copies.append(pltpu.make_async_copy(green_hbm.at[at], out_ref.at[at], sems.at[n]))
         copies[-1].start()
-    tables(freqs_ref, itab_ref, gather_ref)
+    tables(freqs_ref, itab_ref, gather_ref, put_ref)
     for copy in copies:
         copy.wait()
 
@@ -277,8 +277,8 @@
             pair(16 * m + u, pl.multiple_of(m * 9600, 16) + 600 * u)
 
 
-def smooth_kernel(moved_ref, left_ref, gather_ref, out_ref, both, grid, sol, coef_ref):
-    coefficients(left_ref, coef_ref)
+def smooth_kernel(moved_ref, left_ref, put_ref, gather_ref, out_ref, both, grid, sol, coef_ref):
+    coefficients(left_ref, put_ref, coef_ref)
     series = chebyshev_series()
 
     def start(b, _):
@@ -394,9 +394,9 @@
     order = sensor_order.reshape(1, HERE)
     far = lax.ppermute(spectra, AXES, partner(2))
     near = lax.ppermute(spectra, AXES, partner(1))
-    here, itab, gather = call(
+    here, itab, gather, put = call(
         fetch_kernel,
-        [shape(K * HERE * 2, 128), shape(NT, 128), shape(256, 1024)],
+        [shape(K * HERE * 2, 128), shape(NT, 128), shape(256, 1024), shape(2, 1024, 128)],
         [HBM, VMEM],
         [pltpu.SemaphoreType.DMA((4,))],
     )(in_hbm(table), freqs.reshape(1, K))
@@ -422,14 +422,14 @@
     smooth = call(
         smooth_kernel,
         shape(ROWS, 32, 128),
-        [VMEM] * 3,
+        [VMEM] * 4,
         [
             pltpu.VMEM((2, PAR + 2, 4, 8, 128), f32),
             pltpu.VMEM((PAR, 4, 8, 128), f32),
             pltpu.VMEM((PAR * 32, 128), f32),
             pltpu.VMEM((5, 32, 8, 128), f32),
         ],
-    )(moved, left, gather)
+    )(moved, left, put, gather)
     back = lax.all_to_all(smooth, "par", 0, 0, tiled=True)
     out = call(
         inverse_kernel,

time: 81.3 us -> 81.2 us (level)
  no operation moved by 1% of the time
where the time goes in v2:
time: 81.2 us; the launch traced here: 81 us
  blocking collectives  60.4 us (74%)
  Pallas kernels  15.3 us (19%)
  starting transfers between devices  4.4 us (5%)
  waiting for transfers between devices  0.83 us (1%)
    all_to_all x1, blocking collectives, local(): left = lax.all_to_all(sent, 'par', 0, 0, tiled=True)  29.1 us
    all_to_all x1, blocking collectives, local(): lax.all_to_all(summed, AXES, 0, 0, tiled=True, axis_index_groups=groups)  18.9 us
    all_to_all x1, blocking collectives, local(): back = lax.all_to_all(smooth, 'par', 0, 0, tiled=True)  12.4 us
    pallas_call x1, Pallas kernels, local(): call(spectra_kernel, shape(PAD, 128), [HBM, HBM], [pltpu.VMEM((HERE, R, N...  3.73 us
    pallas_call x1, Pallas kernels, local(): call(smooth_kernel, shape(ROWS, 32, 128), [VMEM] * 4, [pltpu.VMEM((2, PAR...  3.56 us
    ppermute x1, starting transfers between devices, local(): far = lax.ppermute(spectra, AXES, partner(2))  3.39 us
    pallas_call x1, Pallas kernels, local(): call(product_kernel, shape(2, PAR, 32, 128), [VMEM] * 3, [pltpu.VMEM((PAR...  3.05 us
    pallas_call x1, Pallas kernels, local(): call(fetch_kernel, [shape(K * HERE * 2, 128), shape(NT, 128), shape(256,...  2.71 us
  transfers between devices with their start and end apart: 5, of which 1 were waited for; matrix products, arithmetic and copies ran while one was open for 0% of the time, Pallas kernels for 4%

profile of v2, /device:TPU:0, one launch (start us, length us, event | category | flops | bytes accessed | tf_op | source)
XLA Modules:
  0.0 81.0 jit_solution(4220108686515402842)
XLA Ops:
  0.0 0.0 copy-start
  0.0 3.7 %shard_map.64.own_ref = bf16[152,128]{1,0:T(8,128)(2,1)S(1)} custom-call(s32[64]{0:T(128)} %freqs_hbm.1, bf16[150,32,420]{2,1,0:T(8,128)(2,1)} %bitcast.15), custom_call_target="tpu_custom_call" | custom-call | tf_op jit(solution)/shard_map/pallas_call | solution.py:382
  3.7 0.1 collective-permute-start.1
  3.8 3.4 %collective-permute-start = (bf16[152,128]{1,0:T(8,128)(2,1)S(1)}, bf16[152,128]{1,0:T(8,128)(2,1)S(1)}, u32[]{:S(2)}, u32[]{:S(2)}) collective-permute-start(bf16[152,128]{1,0:T(8,128)(2,1)S(1)} %shard_map.64.own_ref), channel_id=1, source_target_pairs={{0,64},{1,65},{2,66},{3,67},{4,68},{5,69},{6,70},{7,71},{8,72},{9,... | collective-permute-start | bytes 116744 | tf_op jit(solution)/shard_map/ppermute | solution.py:395
  7.2 0.0 copy-done
  7.2 2.7 %shard_map.65 = (bf16[19200,128]{1,0:T(8,128)(2,1)S(1)}, bf16[420,128]{1,0:T(8,128)(2,1)S(1)}, bf16[256,1024]{1,0:T(8,128)(2,1)S(1)}, bf16[2,1024,128]{2,1,0:T(8,128)(2,1)S(1)}) custom-call(bf16[19200,128]{1,0:T(8,128)(2,1)} %bitcast.14, s32[1,64]{1,0:T(1,128)S(1)} %bitcast.11), custom_call_target="tpu_custom_call" | custom-call | tf_op jit(solution)/shard_map/pallas_call | solution.py:397
  9.9 0.0 collective-permute-done.1.core_ref
  10.0 0.0 collective-permute-done.far_ref
  10.0 0.2 collective-permute-start.2
  10.2 0.0 copy-done.1
  10.2 0.4 collective-permute-start.3
  10.6 0.8 %collective-permute-done.3.other_ref = s32[1,150]{1,0:T(1,128)S(1)} collective-permute-done((s32[1,150]{1,0:T(1,128)S(1)}, s32[1,150]{1,0:T(1,128)S(1)}, u32[]{:S(2)}, u32[]{:S(2)}) %collective-permute-start.3) | collective-permute-done | bytes 632 | tf_op jit(solution)/shard_map/ppermute | solution.py:404
  11.4 0.0 collective-permute-done.2.last_ref
  11.4 0.3 collective-permute-start.4
  11.7 0.0 copy-done.2
  11.7 0.0 copy-done.3
  11.7 0.8 shard_map.66
  12.5 29.1 %all_to_all.15.left_ref = bf16[32,160,128]{2,1,0:T(8,128)(2,1)S(1)} all-to-all(bf16[32,160,128]{2,1,0:T(8,128)(2,1)S(1)} %shard_map.66), channel_id=1, replica_groups=mesh['sens'=4,'par'=32] {'par'}, dimensions={0} | all-to-all | bytes 2621440 | tf_op jit(solution)/shard_map/all_to_all | solution.py:411
  41.6 0.0 collective-permute-done.4.swapped_ref
  41.6 3.0 %shard_map.67 = bf16[2,32,32,128]{3,2,1,0:T(8,128)(2,1)S(1)} custom-call(bf16[32,160,128]{2,1,0:T(8,128)(2,1)S(1)} %all_to_all.15.left_ref, bf16[19200,128]{1,0:T(8,128)(2,1)S(1)} %get-tuple-element.23.green_ref, bf16[19200,128]{1,0:T(8,128)(2,1)S(1)} %collective-permute-done.4.swapped_ref), custom_call_target="tpu_custom_call" | custom-call | tf_op jit(solution)/shard_map/pallas_call | solution.py:412
  44.6 18.9 %all_to_all.16.moved_ref = bf16[64,32,128]{2,1,0:T(8,128)(2,1)S(1)} all-to-all(bf16[64,32,128]{2,1,0:T(8,128)(2,1)S(1)} %bitcast.10), channel_id=1, replica_groups={{0,1,2,3,4,5,6,7,8,9,10,11,12,13,14,15,16,17,18,19,20,21,22,23,24,25,26..., dimensions={0} | all-to-all | bytes 1048576 | tf_op jit(solution)/shard_map/all_to_all | solution.py:421
  63.5 3.6 %shard_map.68 = bf16[32,32,128]{2,1,0:T(8,128)(2,1)S(1)} custom-call(bf16[64,32,128]{2,1,0:T(8,128)(2,1)S(1)} %all_to_all.16.moved_ref, bf16[32,160,128]{2,1,0:T(8,128)(2,1)S(1)} %all_to_all.15.left_ref, bf16[2,1024,128]{2,1,0:T(8,128)(2,1)S(1)} %get-tuple-element.24.put_ref, bf16[256,1024]{1,0:T(8,128)(2,1)S(1)} %get-tuple-element.25.gather_ref), custom_call_target="tpu_custom_call" | custom-call | tf_op jit(solution)/shard_map/pallas_call | solution.py:422
  67.1 12.4 %all_to_all.17.back_ref = bf16[32,32,128]{2,1,0:T(8,128)(2,1)S(1)} all-to-all(bf16[32,32,128]{2,1,0:T(8,128)(2,1)S(1)} %shard_map.68), channel_id=1, replica_groups=mesh['sens'=4,'par'=32] {'par'}, dimensions={0} | all-to-all | bytes 524288 | tf_op jit(solution)/shard_map/all_to_all | solution.py:433
  79.5 1.5 %shard_map.69 = bf16[420,8,128]{2,1,0:T(8,128)(2,1)} custom-call(bf16[32,32,128]{2,1,0:T(8,128)(2,1)S(1)} %all_to_all.17.back_ref, bf16[420,128]{1,0:T(8,128)(2,1)S(1)} %get-tuple-element.26.itab_ref), custom_call_target="tpu_custom_call" | custom-call | tf_op jit(solution)/shard_map/pallas_call | solution.py:434
  (3 shorter events, 0.0 us)
Async XLA Ops:
  0.0 7.2 %copy-start = (s32[64]{0:T(128)S(1)}, s32[64]{0:T(128)}, u32[]{:S(2)}) copy-start(s32[64]{0:T(128)} %freqs_hbm.1) | copy-start | bytes 772
  0.0 10.2 %copy-start.1 = (s32[150]{0:T(256)S(1)}, s32[150]{0:T(256)}, u32[]{:S(2)}) copy-start(s32[150]{0:T(256)} %param.9) | copy-start | bytes 1804
  0.0 11.7 %copy-start.2 = (f32[1,128]{1,0:T(1,128)S(1)}, f32[1,128]{1,0:T(1,128)}, u32[]{:S(2)}) copy-start(f32[1,128]{1,0:T(1,128)} %kappa_ref.1) | copy-start | bytes 1540
  0.0 11.7 %copy-start.3 = (f32[1,128]{1,0:T(1,128)S(1)}, f32[1,128]{1,0:T(1,128)}, u32[]{:S(2)}) copy-start(f32[1,128]{1,0:T(1,128)} %theta_ref.1) | copy-start | bytes 1540
  3.7 6.2 %collective-permute-start.1 = (bf16[152,128]{1,0:T(8,128)(2,1)S(1)}, bf16[152,128]{1,0:T(8,128)(2,1)S(1)}, u32[]{:S(2)}, u32[]{:S(2)}) collective-permute-start(bf16[152,128]{1,0:T(8,128)(2,1)S(1)} %shard_map.64.own_ref), channel_id=1, source_target_pairs={{0,32},{1,33},{2,34},{3,35},{4,36},{5,37},{6,38},{7,39},{8,40},{9,... | collective-permute-start | bytes 116744 | tf_op jit(solution)/shard_map/ppermute | solution.py:396
  3.8 6.1 %collective-permute-start = (bf16[152,128]{1,0:T(8,128)(2,1)S(1)}, bf16[152,128]{1,0:T(8,128)(2,1)S(1)}, u32[]{:S(2)}, u32[]{:S(2)}) collective-permute-start(bf16[152,128]{1,0:T(8,128)(2,1)S(1)} %shard_map.64.own_ref), channel_id=1, source_target_pairs={{0,64},{1,65},{2,66},{3,67},{4,68},{5,69},{6,70},{7,71},{8,72},{9,... | collective-permute-start | bytes 116744 | tf_op jit(solution)/shard_map/ppermute | solution.py:395
  10.0 1.4 %collective-permute-start.2 = (bf16[152,128]{1,0:T(8,128)(2,1)S(1)}, bf16[152,128]{1,0:T(8,128)(2,1)S(1)}, u32[]{:S(2)}, u32[]{:S(2)}) collective-permute-start(bf16[152,128]{1,0:T(8,128)(2,1)S(1)} %collective-permute-done.far_ref), channel_id=1, source_target_pairs={{0,32},{1,33},{2,34},{3,35},{4,36},{5,37},{6,38},{7,39},{8,40},{9,... | collective-permute-start | bytes 116744 | tf_op jit(solution)/shard_map/ppermute | solution.py:405
  10.2 1.2 %collective-permute-start.3 = (s32[1,150]{1,0:T(1,128)S(1)}, s32[1,150]{1,0:T(1,128)S(1)}, u32[]{:S(2)}, u32[]{:S(2)}) collective-permute-start(s32[1,150]{1,0:T(1,128)S(1)} %bitcast.12), channel_id=1, source_target_pairs={{0,32},{1,33},{2,34},{3,35},{4,36},{5,37},{6,38},{7,39},{8,40},{9,... | collective-permute-start | bytes 1808 | tf_op jit(solution)/shard_map/ppermute | solution.py:404
  11.4 30.2 %collective-permute-start.4 = (bf16[19200,128]{1,0:T(8,128)(2,1)S(1)}, bf16[19200,128]{1,0:T(8,128)(2,1)S(1)}, u32[]{:S(2)}, u32[]{:S(2)}) collective-permute-start(bf16[19200,128]{1,0:T(8,128)(2,1)S(1)} %get-tuple-element.23.green_ref), channel_id=1, source_target_pairs={{0,32},{1,33},{2,34},{3,35},{4,36},{5,37},{6,38},{7,39},{8,40},{9,... | collective-permute-start | bytes 14745608 | tf_op jit(solution)/shard_map/ppermute | solution.py:407

commit v3 on v1

--- a/solution.py
+++ b/solution.py
@@ -15,7 +15,8 @@
 SENS = 4
 PAR = 32
 HERE = 150
-PAD = 152
+PAD = 160
+TIMES = 432
 WINDOWS = (0, 128, 344, 472, 256)
 BLOCK = 32 * len(WINDOWS)
 CHUNK = 80
@@ -103,7 +104,7 @@
             y = jnp.sum(y.reshape(count // 2, 4, 8, 128) * own, axis=1)
             parts.append(y.reshape(count // 2 * 8, 128))
         y = jnp.concatenate(parts, axis=0).astype(bf16)
-        rows = -(-count // 8) * 8
+        rows = -(-count // 16) * 16
         y = jnp.dot(fold[:rows, : count * 8], y, preferred_element_type=f32)
         out_ref[n * CHUNK : n * CHUNK + rows, :] = y.astype(bf16)
 
@@ -212,8 +213,8 @@
     twice = jnp.where((iota((K, 128), 1) >> 1) == iota((K, 128), 0), 1.0, 0.0).astype(bf16)
     freqs = jnp.broadcast_to(freqs_ref[...].astype(f32), (8, K)).astype(bf16)
     freq = jnp.dot(freqs, twice, preferred_element_type=f32)[0:1]
-    imag = (iota((NT, 128), 1) & 1) == 1
-    itab_ref[...] = (wave(freq, imag, (NT, 128), 0) * (1.0 / math.sqrt(K))).astype(bf16)
+    imag = (iota((TIMES, 128), 1) & 1) == 1
+    itab_ref[...] = (wave(freq, imag, (TIMES, 128), 0) * (1.0 / math.sqrt(K))).astype(bf16)
 
 
 def fetch_kernel(green_hbm, freqs_ref, out_ref, itab_ref, gather_ref, sems):
@@ -340,15 +341,17 @@
     wide[...] = back_ref[...].reshape(PAR * 32, 128).astype(f32)
     xs = [wide[pl.ds(r, 128, stride=8), :].astype(bf16) for r in range(8)]
     copies = []
-    for n, (start, count) in enumerate(((0, 144), (144, 144), (288, 132))):
-        at = pl.ds(start, count)
+    step = TIMES // 3
+    for n in range(3):
+        at = pl.ds(n * step, step)
         itab = itab_ref[at, :]
         for r in range(8):
             y = jnp.dot(itab, xs[r], preferred_element_type=f32)
-            mixed[pl.ds(8 * start + r, count, stride=8), :] = y
-        y = mixed[8 * start : 8 * (start + count), :].astype(bf16)
-        ready[at] = y.reshape(count, 8, 128)
-        copies.append(pltpu.make_async_copy(ready.at[at], out_hbm.at[at], sems.at[n]))
+            mixed[pl.ds(8 * n * step + r, step, stride=8), :] = y
+        y = mixed[8 * n * step : 8 * (n + 1) * step, :].astype(bf16)
+        ready[at] = y.reshape(step, 8, 128)
+        used = pl.ds(n * step, min(step, NT - n * step))
+        copies.append(pltpu.make_async_copy(ready.at[used], out_hbm.at[used], sems.at[n]))
         copies[-1].start()
     for copy in copies:
         copy.wait()
@@ -396,7 +399,7 @@
     near = lax.ppermute(spectra, AXES, partner(1))
     here, itab, gather = call(
         fetch_kernel,
-        [shape(K * HERE * 2, 128), shape(NT, 128), shape(256, 1024)],
+        [shape(K * HERE * 2, 128), shape(TIMES, 128), shape(256, 1024)],
         [HBM, VMEM],
         [pltpu.SemaphoreType.DMA((4,))],
     )(in_hbm(table), freqs.reshape(1, K))
@@ -437,8 +440,8 @@
         [VMEM, VMEM],
         [
             pltpu.VMEM((PAR * 32, 128), f32),
-            pltpu.VMEM((NT * 8, 128), f32),
-            pltpu.VMEM((NT, 8, 128), bf16),
+            pltpu.VMEM((TIMES * 8, 128), f32),
+            pltpu.VMEM((TIMES, 8, 128), bf16),
             pltpu.SemaphoreType.DMA((3,)),
         ],
         to=HBM,

time: 81.3 us -> 81.3 us (level)
  no operation moved by 1% of the time
where the time goes in v3:
time: 81.3 us; the launch traced here: 81.1 us
  blocking collectives  60.6 us (75%)
  Pallas kernels  15.1 us (19%)
  starting transfers between devices  4.4 us (5%)
  waiting for transfers between devices  0.83 us (1%)
    all_to_all x1, blocking collectives, local(): left = lax.all_to_all(sent, 'par', 0, 0, tiled=True)  29.3 us
    all_to_all x1, blocking collectives, local(): lax.all_to_all(summed, AXES, 0, 0, tiled=True, axis_index_groups=groups)  18.9 us
    all_to_all x1, blocking collectives, local(): back = lax.all_to_all(smooth, 'par', 0, 0, tiled=True)  12.4 us
    pallas_call x1, Pallas kernels, local(): call(spectra_kernel, shape(PAD, 128), [HBM, HBM], [pltpu.VMEM((HERE, R, N...  3.73 us
    pallas_call x1, Pallas kernels, local(): call(smooth_kernel, shape(ROWS, 32, 128), [VMEM] * 3, [pltpu.VMEM((2, PAR...  3.65 us
    ppermute x1, starting transfers between devices, local(): far = lax.ppermute(spectra, AXES, partner(2))  3.39 us
    pallas_call x1, Pallas kernels, local(): call(product_kernel, shape(2, PAR, 32, 128), [VMEM] * 3, [pltpu.VMEM((PAR...  3.07 us
    pallas_call x1, Pallas kernels, local(): call(fetch_kernel, [shape(K * HERE * 2, 128), shape(TIMES, 128), shape(25...  2.46 us
  transfers between devices with their start and end apart: 5, of which 1 were waited for; matrix products, arithmetic and copies ran while one was open for 0% of the time, Pallas kernels for 4%

profile of v3, /device:TPU:0, one launch (start us, length us, event | category | flops | bytes accessed | tf_op | source)
XLA Modules:
  0.0 81.1 jit_solution(11607141545116552913)
XLA Ops:
  0.0 0.0 copy-start
  0.0 3.7 %shard_map.64.own_ref = bf16[160,128]{1,0:T(8,128)(2,1)S(1)} custom-call(s32[64]{0:T(128)} %freqs_hbm.1, bf16[150,32,420]{2,1,0:T(8,128)(2,1)} %bitcast.14), custom_call_target="tpu_custom_call" | custom-call | tf_op jit(solution)/shard_map/pallas_call | solution.py:385
  3.7 0.1 collective-permute-start.1
  3.8 3.4 %collective-permute-start = (bf16[160,128]{1,0:T(8,128)(2,1)S(1)}, bf16[160,128]{1,0:T(8,128)(2,1)S(1)}, u32[]{:S(2)}, u32[]{:S(2)}) collective-permute-start(bf16[160,128]{1,0:T(8,128)(2,1)S(1)} %shard_map.64.own_ref), channel_id=1, source_target_pairs={{0,64},{1,65},{2,66},{3,67},{4,68},{5,69},{6,70},{7,71},{8,72},{9,... | collective-permute-start | bytes 122888 | tf_op jit(solution)/shard_map/ppermute | solution.py:398
  7.2 0.0 copy-done
  7.2 2.5 %shard_map.65 = (bf16[19200,128]{1,0:T(8,128)(2,1)S(1)}, bf16[432,128]{1,0:T(8,128)(2,1)S(1)}, bf16[256,1024]{1,0:T(8,128)(2,1)S(1)}) custom-call(bf16[19200,128]{1,0:T(8,128)(2,1)} %bitcast.15, s32[1,64]{1,0:T(1,128)S(1)} %bitcast.11), custom_call_target="tpu_custom_call" | custom-call | tf_op jit(solution)/shard_map/pallas_call | solution.py:400
  9.7 0.0 collective-permute-done.1.core_ref
  9.7 0.0 collective-permute-done.far_ref
  9.7 0.2 collective-permute-start.2
  9.9 0.0 copy-done.1
  9.9 0.4 collective-permute-start.3
  10.3 0.8 %collective-permute-done.3.other_ref = s32[1,150]{1,0:T(1,128)S(1)} collective-permute-done((s32[1,150]{1,0:T(1,128)S(1)}, s32[1,150]{1,0:T(1,128)S(1)}, u32[]{:S(2)}, u32[]{:S(2)}) %collective-permute-start.3) | collective-permute-done | bytes 632 | tf_op jit(solution)/shard_map/ppermute | solution.py:407
  11.1 0.0 collective-permute-done.2.last_ref
  11.1 0.3 collective-permute-start.4
  11.5 0.0 copy-done.2
  11.5 0.0 copy-done.3
  11.5 0.8 shard_map.66
  12.3 29.3 %all_to_all.15.left_ref = bf16[32,160,128]{2,1,0:T(8,128)(2,1)S(1)} all-to-all(bf16[32,160,128]{2,1,0:T(8,128)(2,1)S(1)} %shard_map.66), channel_id=1, replica_groups=mesh['sens'=4,'par'=32] {'par'}, dimensions={0} | all-to-all | bytes 2621440 | tf_op jit(solution)/shard_map/all_to_all | solution.py:414
  41.6 0.0 collective-permute-done.4.swapped_ref
  41.6 3.1 %shard_map.67 = bf16[2,32,32,128]{3,2,1,0:T(8,128)(2,1)S(1)} custom-call(bf16[32,160,128]{2,1,0:T(8,128)(2,1)S(1)} %all_to_all.15.left_ref, bf16[19200,128]{1,0:T(8,128)(2,1)S(1)} %get-tuple-element.22.green_ref, bf16[19200,128]{1,0:T(8,128)(2,1)S(1)} %collective-permute-done.4.swapped_ref), custom_call_target="tpu_custom_call" | custom-call | tf_op jit(solution)/shard_map/pallas_call | solution.py:415
  44.7 18.9 %all_to_all.16.moved_ref = bf16[64,32,128]{2,1,0:T(8,128)(2,1)S(1)} all-to-all(bf16[64,32,128]{2,1,0:T(8,128)(2,1)S(1)} %bitcast.10), channel_id=1, replica_groups={{0,1,2,3,4,5,6,7,8,9,10,11,12,13,14,15,16,17,18,19,20,21,22,23,24,25,26..., dimensions={0} | all-to-all | bytes 1048576 | tf_op jit(solution)/shard_map/all_to_all | solution.py:424
  63.5 3.6 %shard_map.68 = bf16[32,32,128]{2,1,0:T(8,128)(2,1)S(1)} custom-call(bf16[64,32,128]{2,1,0:T(8,128)(2,1)S(1)} %all_to_all.16.moved_ref, bf16[32,160,128]{2,1,0:T(8,128)(2,1)S(1)} %all_to_all.15.left_ref, bf16[256,1024]{1,0:T(8,128)(2,1)S(1)} %get-tuple-element.23.gather_ref), custom_call_target="tpu_custom_call" | custom-call | tf_op jit(solution)/shard_map/pallas_call | solution.py:425
  67.2 12.4 %all_to_all.17.back_ref = bf16[32,32,128]{2,1,0:T(8,128)(2,1)S(1)} all-to-all(bf16[32,32,128]{2,1,0:T(8,128)(2,1)S(1)} %shard_map.68), channel_id=1, replica_groups=mesh['sens'=4,'par'=32] {'par'}, dimensions={0} | all-to-all | bytes 524288 | tf_op jit(solution)/shard_map/all_to_all | solution.py:436
  79.6 1.5 %shard_map.69 = bf16[420,8,128]{2,1,0:T(8,128)(2,1)} custom-call(bf16[32,32,128]{2,1,0:T(8,128)(2,1)S(1)} %all_to_all.17.back_ref, bf16[432,128]{1,0:T(8,128)(2,1)S(1)} %get-tuple-element.24.itab_ref), custom_call_target="tpu_custom_call" | custom-call | tf_op jit(solution)/shard_map/pallas_call | solution.py:437
  (3 shorter events, 0.0 us)
Async XLA Ops:
  0.0 7.2 %copy-start = (s32[64]{0:T(128)S(1)}, s32[64]{0:T(128)}, u32[]{:S(2)}) copy-start(s32[64]{0:T(128)} %freqs_hbm.1) | copy-start | bytes 772
  0.0 9.9 %copy-start.1 = (s32[150]{0:T(256)S(1)}, s32[150]{0:T(256)}, u32[]{:S(2)}) copy-start(s32[150]{0:T(256)} %param.9) | copy-start | bytes 1804
  0.0 11.5 %copy-start.2 = (f32[1,128]{1,0:T(1,128)S(1)}, f32[1,128]{1,0:T(1,128)}, u32[]{:S(2)}) copy-start(f32[1,128]{1,0:T(1,128)} %kappa_ref.1) | copy-start | bytes 1540
  0.0 11.5 %copy-start.3 = (f32[1,128]{1,0:T(1,128)S(1)}, f32[1,128]{1,0:T(1,128)}, u32[]{:S(2)}) copy-start(f32[1,128]{1,0:T(1,128)} %theta_ref.1) | copy-start | bytes 1540
  3.7 5.9 %collective-permute-start.1 = (bf16[160,128]{1,0:T(8,128)(2,1)S(1)}, bf16[160,128]{1,0:T(8,128)(2,1)S(1)}, u32[]{:S(2)}, u32[]{:S(2)}) collective-permute-start(bf16[160,128]{1,0:T(8,128)(2,1)S(1)} %shard_map.64.own_ref), channel_id=1, source_target_pairs={{0,32},{1,33},{2,34},{3,35},{4,36},{5,37},{6,38},{7,39},{8,40},{9,... | collective-permute-start | bytes 122888 | tf_op jit(solution)/shard_map/ppermute | solution.py:399
  3.8 5.9 %collective-permute-start = (bf16[160,128]{1,0:T(8,128)(2,1)S(1)}, bf16[160,128]{1,0:T(8,128)(2,1)S(1)}, u32[]{:S(2)}, u32[]{:S(2)}) collective-permute-start(bf16[160,128]{1,0:T(8,128)(2,1)S(1)} %shard_map.64.own_ref), channel_id=1, source_target_pairs={{0,64},{1,65},{2,66},{3,67},{4,68},{5,69},{6,70},{7,71},{8,72},{9,... | collective-permute-start | bytes 122888 | tf_op jit(solution)/shard_map/ppermute | solution.py:398
  9.7 1.4 %collective-permute-start.2 = (bf16[160,128]{1,0:T(8,128)(2,1)S(1)}, bf16[160,128]{1,0:T(8,128)(2,1)S(1)}, u32[]{:S(2)}, u32[]{:S(2)}) collective-permute-start(bf16[160,128]{1,0:T(8,128)(2,1)S(1)} %collective-permute-done.far_ref), channel_id=1, source_target_pairs={{0,32},{1,33},{2,34},{3,35},{4,36},{5,37},{6,38},{7,39},{8,40},{9,... | collective-permute-start | bytes 122888 | tf_op jit(solution)/shard_map/ppermute | solution.py:408
  9.9 1.2 %collective-permute-start.3 = (s32[1,150]{1,0:T(1,128)S(1)}, s32[1,150]{1,0:T(1,128)S(1)}, u32[]{:S(2)}, u32[]{:S(2)}) collective-permute-start(s32[1,150]{1,0:T(1,128)S(1)} %bitcast.12), channel_id=1, source_target_pairs={{0,32},{1,33},{2,34},{3,35},{4,36},{5,37},{6,38},{7,39},{8,40},{9,... | collective-permute-start | bytes 1808 | tf_op jit(solution)/shard_map/ppermute | solution.py:407
  11.1 30.5 %collective-permute-start.4 = (bf16[19200,128]{1,0:T(8,128)(2,1)S(1)}, bf16[19200,128]{1,0:T(8,128)(2,1)S(1)}, u32[]{:S(2)}, u32[]{:S(2)}) collective-permute-start(bf16[19200,128]{1,0:T(8,128)(2,1)S(1)} %get-tuple-element.22.green_ref), channel_id=1, source_target_pairs={{0,32},{1,33},{2,34},{3,35},{4,36},{5,37},{6,38},{7,39},{8,40},{9,... | collective-permute-start | bytes 14745608 | tf_op jit(solution)/shard_map/ppermute | solution.py:410
